TPU v7x, 256 devices: a whole 4x4x8 slice. The times are simulated.
256 devices in a mesh: section: 8 (over z_hi, x), seq: 32 (over y, z_lo, core).
Axes of the slice: x: 4, y: 4, z: 8 (z_hi: 2, z_lo: 4; z = z_hi * 4 + z_lo), core: 2. Of those that a mesh axis runs over, the one named last changes fastest.
Arguments:
- input_keys: bfloat16 [8, 16384, 2048], P('section', 'seq'), may hold values from -6 to 6
- input_values: bfloat16 [8, 16384, 2048], P('section', 'seq'), may hold values from -6 to 6
- latent_queries: bfloat16 [8, 1024, 2048], P('section', 'seq'), may hold values from -6 to 6
- forward_out: bfloat16 [8, 1024, 2048], P('section', 'seq'), may hold values from -0.59765625 to 0.59765625
- log_norms: float32 [8, 1024, 16], P('section'), as said below
- block_table: int32 [8, 8], P('section'), may hold values from 0 to 127, as said below
- layer_grads: float32 [8, 8, 1024, 2048], P('section', None, 'seq'), may hold values from -600 to 600
Outputs:
- grad_keys: bfloat16 [8, 16384, 2048], P('section', 'seq')
- grad_values: bfloat16 [8, 16384, 2048], P('section', 'seq')
- grad_queries: bfloat16 [8, 1024, 2048], P('section', 'seq')
Inputs may be any that keep to these rules, and one draw needn't show every extreme that they name: block_table[b, a] is the last block of 128 input positions that latent block a sees; it rises strictly with a, it lies from 16 * (a + 1) - 8 to 16 * (a + 1) - 1, and the last latent block sees every position. log_norms[b, i, h] stand in for the saved normalizers: they are drawn near the log of the number of positions that latent i sees, plus 0.5, with noise of at most 0.45 either way.
All inputs are finite; a program needn't handle non-finite values.
Results may differ from a plain program's by a relative error of at most 0.0058.
Values may be sent and summed in bfloat16 or wider, within the bound.
No kernel may reach another device: no remote copies, remote signals or barrier semaphores. Data moves between devices by JAX's collectives and lax.ppermute only.
A program may use at most 128 MiB of HBM per device.

v0:
```python
import math
import jax
import jax.numpy as jnp
from jax import lax
from jax.sharding import PartitionSpec as P

BLK = 128


def body(
    input_keys, input_values, latent_queries, forward_out, log_norms, block_table, layer_grads
):
    arrived = lax.psum_scatter(layer_grads, "section", scatter_dimension=1, tiled=True)
    out_grad = arrived[0, 0].astype(jnp.bfloat16)
    head_count = log_norms.shape[2]
    width = input_keys.shape[2]
    head_dim = width // head_count
    score_scale = 1.0 / math.sqrt(head_dim)
    tok_count = input_keys.shape[1]
    limits = jnp.repeat(block_table[0], BLK)
    unit = lax.axis_index("seq")
    key_block = (unit * tok_count + jnp.arange(tok_count)) // BLK
    key_heads = input_keys[0].reshape(tok_count, head_count, head_dim).transpose(1, 0, 2)
    val_heads = input_values[0].reshape(tok_count, head_count, head_dim).transpose(1, 0, 2)
    lat_stack = jnp.stack([latent_queries[0], out_grad, forward_out[0]])
    all_lse = log_norms[0]
    lat_total = all_lse.shape[0]
    zeros_tok = jnp.zeros((head_count, tok_count, head_dim), jnp.float32)
    zeros_lat = jnp.zeros((lat_total, head_count, head_dim), jnp.float32)
    totals = (zeros_tok, zeros_tok, zeros_lat)
    latent_piece = lax.all_gather(lat_stack, "seq", axis=1, tiled=True)
    row_count = latent_piece.shape[1]
    step_rows = math.gcd(row_count, 256)
    step_count = row_count // step_rows
    split = latent_piece.reshape(3, step_count, step_rows, head_count, head_dim).transpose(
        1, 0, 2, 3, 4
    )

    def row_step(carry, inputs):
        key_total, value_total, query_total = carry
        lat_block, step_index = inputs
        row_start = step_index * step_rows
        queries = lat_block[0]
        grads = lat_block[1]
        lse_rows = lax.dynamic_slice_in_dim(all_lse, row_start, step_rows, 0)
        lim_rows = lax.dynamic_slice_in_dim(limits, row_start, step_rows, 0)
        visible = key_block[None, :] <= lim_rows[:, None]
        delta = jnp.sum(grads.astype(jnp.float32) * lat_block[2].astype(jnp.float32), axis=2)
        scores = (
            jnp.einsum("ihc,hjc->hij", queries, key_heads, preferred_element_type=jnp.float32)
            * score_scale
        )
        probs = jnp.where(visible[None], jnp.exp(scores - lse_rows.T[:, :, None]), 0.0)
        probs_low = probs.astype(jnp.bfloat16)
        dprobs = jnp.einsum("ihc,hjc->hij", grads, val_heads, preferred_element_type=jnp.float32)
        dscores = (probs * (dprobs - delta.T[:, :, None])).astype(jnp.bfloat16)
        query_part = jnp.einsum(
            "hij,hjc->ihc", dscores, key_heads, preferred_element_type=jnp.float32
        )
        key_total = key_total + jnp.einsum(
            "hij,ihc->hjc", dscores, queries, preferred_element_type=jnp.float32
        )
        value_total = value_total + jnp.einsum(
            "hij,ihc->hjc", probs_low, grads, preferred_element_type=jnp.float32
        )
        old_rows = lax.dynamic_slice_in_dim(query_total, row_start, step_rows, 0)
        query_total = lax.dynamic_update_slice_in_dim(
            query_total, old_rows + query_part, row_start, 0
        )
        return ((key_total, value_total, query_total), None)

    totals, ignored = lax.scan(row_step, totals, (split, jnp.arange(step_count, dtype=jnp.int32)))
    key_total, value_total, query_total = totals
    grad_k = (
        (key_total * score_scale).astype(jnp.bfloat16).transpose(1, 0, 2).reshape(tok_count, width)
    )
    grad_v = value_total.astype(jnp.bfloat16).transpose(1, 0, 2).reshape(tok_count, width)
    query_rows = lax.psum_scatter(
        query_total.reshape(lat_total, width) * score_scale, "seq", scatter_dimension=0, tiled=True
    )
    grad_q = query_rows.astype(jnp.bfloat16)
    return (grad_k[None], grad_v[None], grad_q[None])


def solution(mesh):
    placed = (
        P("section", "seq", None),
        P("section", "seq", None),
        P("section", "seq", None),
        P("section", "seq", None),
        P("section", None, None),
        P("section", None),
        P("section", None, "seq", None),
    )
    return jax.shard_map(
        body,
        mesh=mesh,
        in_specs=placed,
        out_specs=(P("section", "seq", None), P("section", "seq", None), P("section", "seq", None)),
        check_vma=False,
    )
```

profile of v0, /device:TPU:2, one launch (start us, length us, event | category | flops | bytes accessed | tf_op | source)
XLA Modules:
  0.0 489.3 jit_solution(8766786200359334464)
XLA Ops:
  8.0 102.2 %reduce-scatter.3.cloned.1.call-done = f32[1,1,32,2048]{3,2,1,0:T(8,128)} async-done(((f32[1,8,32,2048]{3,2,1,0:T(8,128)}), f32[1,1,32,2048]{3,2,1,0:T(8,128)}) %reduce-scatter.3.cloned.1.call-update) | async-done | bytes 262160 | tf_op jit(solution)/shard_map/reduce_scatter | solution.py:13
  118.6 4.0 copy.18
  122.5 3.9 copy.21
  126.5 61.8 %all-gather.2.cloned.1.call-done = bf16[3,1024,2048]{2,1,0:T(8,128)(2,1)} async-done(((bf16[3,32,2048]{2,1,0:T(8,128)(2,1)}), bf16[3,1024,2048]{2,1,0:T(8,128)(2,1)}) %all-gather.2.cloned.1.call-update) | async-done | bytes 12582928 | tf_op jit(solution)/shard_map/all_gather | solution.py:31
  188.3 11.4 %copy.32 = bf16[384,8,16,128]{3,2,1,0:T(8,128)(2,1)} copy(bf16[384,8,16,128]{3,1,2,0:T(8,128)(2,1)} %bitcast.89) | data formatting | bytes 25165824
  199.8 4.1 broadcast_in_dim.30
  203.8 106.4 %while.15 = (s32[]{:T(128)}, f32[16,512,128]{2,1,0:T(8,128)}, f32[16,512,128]{2,1,0:T(8,128)}, f32[1024,16,128]{2,0,1:T(8,128)}, s32[4]{0:T(128)S(1)}, /*index=5...) while((s32[]{:T(128)}, f32[16,512,128]{2,1,0:T(8,128)}, ...), condition=%wide.region_3.4_spmd.clone, body=%wide.region_1.3_spmd.clone.sunk | while | flops 2712276992 | bytes 86482224 | solution.py:72
  210.8 3.8 multiply_convert_fusion.3
  214.6 5.0 %select_add_fusion.5 = f32[16,512,128]{2,1,0:T(8,128)} fusion(f32[16,512,128]{2,1,0:T(8,128)} %get-tuple-element.234, pred[]{:T(512)S(6)} %compare.5, f32[16,256,512]{2,1,0:T(8,128)S(1)} %fusion.40, f32[16,256]{1,0:T(8,128)S(1)} %dynamic-slice_bitcast_fusion.2, pred[256,512]{1,0:T(8,128)(4,1)S(1)} %broadcast_compare_fusion.2, ...), kind=kOutput, calls=%fused_computation.5.clone.1 | convolution fusion | flops 547356672 | bytes 17973248 | tf_op jit(solution)/shard_map/while/body/eval_jaxpr/hij,ihc->hjc/dot_general | solution.py:63
  223.3 4.3 fusion.42
  234.7 3.8 multiply_convert_fusion.3
  238.5 6.6 %select_add_fusion.5 = f32[16,512,128]{2,1,0:T(8,128)} fusion(f32[16,512,128]{2,1,0:T(8,128)} %get-tuple-element.234, pred[]{:T(512)S(6)} %compare.5, f32[16,256,512]{2,1,0:T(8,128)S(1)} %fusion.40, f32[16,256]{1,0:T(8,128)S(1)} %dynamic-slice_bitcast_fusion.2, pred[256,512]{1,0:T(8,128)(4,1)S(1)} %broadcast_compare_fusion.2, ...), kind=kOutput, calls=%fused_computation.5.clone.1 | convolution fusion | flops 547356672 | bytes 17973248 | tf_op jit(solution)/shard_map/while/body/eval_jaxpr/hij,ihc->hjc/dot_general | solution.py:63
  245.0 5.8 %select_add_fusion.4 = f32[16,512,128]{2,1,0:T(8,128)} fusion(f32[16,512,128]{2,1,0:T(8,128)} %get-tuple-element.233, bf16[16,256,512]{2,1,0:T(8,128)(2,1)S(1)} %multiply_convert_fusion.3, pred[]{:T(512)S(6)} %compare.5, bf16[1,1,256,16,128]{4,3,2,0,1:T(8,128)(2,1)S(1)} %get-tuple-element.212), kind=kOutput, calls=%fused_computation.6.clone.1 | convolution fusion | flops 538968064 | bytes 13631489 | tf_op jit(solution)/shard_map/while/body/eval_jaxpr/hij,ihc->hjc/dot_general | solution.py:60
  250.9 4.3 fusion.42
  265.9 6.6 %select_add_fusion.5 = f32[16,512,128]{2,1,0:T(8,128)} fusion(f32[16,512,128]{2,1,0:T(8,128)} %get-tuple-element.234, pred[]{:T(512)S(6)} %compare.5, f32[16,256,512]{2,1,0:T(8,128)S(1)} %fusion.40, f32[16,256]{1,0:T(8,128)S(1)} %dynamic-slice_bitcast_fusion.2, pred[256,512]{1,0:T(8,128)(4,1)S(1)} %broadcast_compare_fusion.2, ...), kind=kOutput, calls=%fused_computation.5.clone.1 | convolution fusion | flops 547356672 | bytes 17973248 | tf_op jit(solution)/shard_map/while/body/eval_jaxpr/hij,ihc->hjc/dot_general | solution.py:63
  272.5 5.8 %select_add_fusion.4 = f32[16,512,128]{2,1,0:T(8,128)} fusion(f32[16,512,128]{2,1,0:T(8,128)} %get-tuple-element.233, bf16[16,256,512]{2,1,0:T(8,128)(2,1)S(1)} %multiply_convert_fusion.3, pred[]{:T(512)S(6)} %compare.5, bf16[1,1,256,16,128]{4,3,2,0,1:T(8,128)(2,1)S(1)} %get-tuple-element.212), kind=kOutput, calls=%fused_computation.6.clone.1 | convolution fusion | flops 538968064 | bytes 13631489 | tf_op jit(solution)/shard_map/while/body/eval_jaxpr/hij,ihc->hjc/dot_general | solution.py:60
  278.4 4.4 fusion.42
  289.8 3.8 multiply_convert_fusion.3
  293.6 6.6 %select_add_fusion.5 = f32[16,512,128]{2,1,0:T(8,128)} fusion(f32[16,512,128]{2,1,0:T(8,128)} %get-tuple-element.234, pred[]{:T(512)S(6)} %compare.5, f32[16,256,512]{2,1,0:T(8,128)S(1)} %fusion.40, f32[16,256]{1,0:T(8,128)S(1)} %dynamic-slice_bitcast_fusion.2, pred[256,512]{1,0:T(8,128)(4,1)S(1)} %broadcast_compare_fusion.2, ...), kind=kOutput, calls=%fused_computation.5.clone.1 | convolution fusion | flops 547356672 | bytes 17973248 | tf_op jit(solution)/shard_map/while/body/eval_jaxpr/hij,ihc->hjc/dot_general | solution.py:63
  300.1 5.8 %select_add_fusion.4 = f32[16,512,128]{2,1,0:T(8,128)} fusion(f32[16,512,128]{2,1,0:T(8,128)} %get-tuple-element.233, bf16[16,256,512]{2,1,0:T(8,128)(2,1)S(1)} %multiply_convert_fusion.3, pred[]{:T(512)S(6)} %compare.5, bf16[1,1,256,16,128]{4,3,2,0,1:T(8,128)(2,1)S(1)} %get-tuple-element.212), kind=kOutput, calls=%fused_computation.6.clone.1 | convolution fusion | flops 538968064 | bytes 13631489 | tf_op jit(solution)/shard_map/while/body/eval_jaxpr/hij,ihc->hjc/dot_general | solution.py:60
  306.0 4.3 fusion.42
  310.2 7.9 %copy_bitcast_fusion.7 = f32[1024,2048]{1,0:T(8,128)} fusion(f32[1024,16,128]{2,0,1:T(8,128)} %get-tuple-element.64), kind=kLoop, calls=%fused_computation.35 | loop fusion | flops 2097152 | bytes 16777216 | tf_op jit(solution)/shard_map/mul | solution.py:79
  318.1 5.9 %fusion.19 = (bf16[512,16,128]{2,0,1:T(8,128)(2,1)S(1)}, bf16[512,16,128]{2,0,1:T(8,128)(2,1)}) fusion(f32[16,512,128]{2,1,0:T(8,128)} %get-tuple-element.62, f32[16,512,128]{2,1,0:T(8,128)} %get-tuple-element.63), kind=kLoop, calls=%fused_computation.38 | loop fusion | flops 3145728 | bytes 12582912 | tf_op jit(solution)/shard_map/transpose | solution.py:75
  332.9 148.2 %reduce-scatter.5.cloned.1.call-done = f32[32,2048]{1,0:T(8,128)} async-done(((f32[1024,2048]{1,0:T(8,128)}), f32[32,2048]{1,0:T(8,128)}) %reduce-scatter.5.cloned.1.call-update) | async-done | bytes 262160 | tf_op jit(solution)/shard_map/reduce_scatter | solution.py:78
  (67 shorter events, 52.5 us)
Async XLA Ops:
  7.2 119.3 %copy-start = (s32[1,8]{1,0:T(1,128)S(1)}, s32[1,8]{1,0:T(1,128)}, u32[]{:S(2)}) copy-start(s32[1,8]{1,0:T(1,128)} %param.14) | copy-start | bytes 100
  7.2 105.9 %copy-start.2 = (bf16[1,512,2048]{2,1,0:T(8,128)(2,1)S(1)}, bf16[1,512,2048]{2,1,0:T(8,128)(2,1)}, u32[]{:S(2)}) copy-start(bf16[1,512,2048]{2,1,0:T(8,128)(2,1)} %param.9) | copy-start | bytes 6291460
  7.2 103.0 %reduce-scatter.3.cloned.1.call-start = ((), (), s32[]{:S(2)}) async-start(), calls=%async_computation.2 | async-start | bytes 2359296 | tf_op jit(solution)/shard_map/reduce_scatter | solution.py:13
  7.9 180.4 %all-gather.2.cloned.1.call-start = ((), (), s32[]{:S(2)}) async-start(), calls=%async_computation.3 | async-start | bytes 12976128 | tf_op jit(solution)/shard_map/all_gather | solution.py:31
  113.0 368.2 %reduce-scatter.5.cloned.1.call-start = ((), (), s32[]{:S(2)}) async-start(), calls=%async_computation.4 | async-start | bytes 8650752 | tf_op jit(solution)/shard_map/reduce_scatter | solution.py:78
  209.2 1.6 copy-start.3
  233.1 1.6 copy-start.3
  260.6 1.6 copy-start.3
  288.2 1.6 copy-start.3
  327.7 155.1 %copy-start.1 = (s32[1,8]{1,0:T(1,128)S(1)}, s32[1,8]{1,0:T(1,128)}, u32[]{:S(2)}) copy-start(s32[1,8]{1,0:T(1,128)} %param.14) | copy-start | bytes 100
Sparse Core Ops, SparseCore 0:
  12.1 98.0 reduce-scatter.2
  113.1 75.1 all-gather.1
  318.3 162.8 reduce-scatter.4
where the time goes:
time: 490 us; the launch traced here: 489 us
  waiting for transfers between devices  313 us (64%)
  matrix products  83.4 us (17%)
  local copies, waits for them, and re-layouts  54.4 us (11%)
  other arithmetic  22 us (4%)
  between operations  13.8 us (3%)
    reduce_scatter x1, waiting for transfers between devices, body(): lax.psum_scatter(query_total.reshape(lat_total, width) * score_scale, 'se...  148 us
    reduce_scatter x1, waiting for transfers between devices, body(): lax.psum_scatter(layer_grads, 'section', scatter_dimension=1, tiled=True)  102 us
    all_gather x1, waiting for transfers between devices, body(): latent_piece = lax.all_gather(lat_stack, 'seq', axis=1, tiled=True)  61.8 us
    unnamed x11, local copies, waits for them, and re-layouts  24.8 us
    dot_general x4, matrix products, row_step(): jnp.einsum('hij,ihc->hjc', probs_low, grads, preferred_element_type=jnp.f...  24.8 us
    dot_general x4, matrix products, row_step(): jnp.einsum('hij,ihc->hjc', dscores, queries, preferred_element_type=jnp.f...  21.2 us
    dot_general x4, matrix products, row_step(): jnp.einsum('hij,hjc->ihc', dscores, key_heads, preferred_element_type=jnp...  17.3 us
    dot_general x4, matrix products, row_step(): jnp.einsum('ihc,hjc->hij', grads, val_heads, preferred_element_type=jnp.f...  15.1 us
  transfers between devices with their start and end apart: 3, of which 3 were waited for; matrix products, arithmetic and copies ran while one was open for 6% of the time, Pallas kernels for 0%

commit v1 on v0

--- a/solution.py
+++ b/solution.py
@@ -5,6 +5,11 @@
 from jax.sharding import PartitionSpec as P
 
 BLK = 128
+
+
+def swapped_in(shard, axis, dim):
+    sent = jnp.stack([shard] * lax.axis_size(axis))
+    return jnp.concatenate(lax.all_to_all(sent, axis, 0, 0), axis=dim)
 
 
 def body(
@@ -28,7 +33,7 @@
     zeros_tok = jnp.zeros((head_count, tok_count, head_dim), jnp.float32)
     zeros_lat = jnp.zeros((lat_total, head_count, head_dim), jnp.float32)
     totals = (zeros_tok, zeros_tok, zeros_lat)
-    latent_piece = lax.all_gather(lat_stack, "seq", axis=1, tiled=True)
+    latent_piece = swapped_in(lat_stack, "seq", 1)
     row_count = latent_piece.shape[1]
     step_rows = math.gcd(row_count, 256)
     step_count = row_count // step_rows

time: 490 us -> 698 us (1.42)
  waiting for transfers between devices: 313 us -> 508 us
  local copies, waits for them, and re-layouts: 54.4 us -> 61.7 us
    all_to_all x0 -> x1, waiting for transfers between devices: none -> 262 us  [swapped_in(): return jnp.concatenate(lax.all_to_all(sent, axis, 0, 0), axis=dim)]
    all_gather x1 -> x0, waiting for transfers between devices: 61.8 us -> none  [body(): latent_piece = lax.all_gather(lat_stack, 'seq', axis=1, tiled=True)]
  transfers between devices with their start and end apart: 3 -> 3, of which waited for: 3 -> 3; matrix products, arithmetic and copies ran while one was open for 6% -> 4% of each run, Pallas kernels for 0% -> 0%
where the time goes in v1:
time: 698 us; the launch traced here: 697 us
  waiting for transfers between devices  508 us (73%)
  matrix products  83.5 us (12%)
  local copies, waits for them, and re-layouts  61.7 us (9%)
  other arithmetic  21.2 us (3%)
  between operations  14.1 us (2%)
    all_to_all x1, waiting for transfers between devices, swapped_in(): return jnp.concatenate(lax.all_to_all(sent, axis, 0, 0), axis=dim)  262 us
    reduce_scatter x1, waiting for transfers between devices, body(): lax.psum_scatter(query_total.reshape(lat_total, width) * score_scale, 'se...  144 us
    reduce_scatter x1, waiting for transfers between devices, body(): lax.psum_scatter(layer_grads, 'section', scatter_dimension=1, tiled=True)  102 us
    dot_general x4, matrix products, row_step(): jnp.einsum('hij,ihc->hjc', probs_low, grads, preferred_element_type=jnp.f...  24.8 us
    dot_general x4, matrix products, row_step(): jnp.einsum('hij,ihc->hjc', dscores, queries, preferred_element_type=jnp.f...  21.2 us
    unnamed x11, local copies, waits for them, and re-layouts  19.9 us
    dot_general x4, matrix products, row_step(): jnp.einsum('hij,hjc->ihc', dscores, key_heads, preferred_element_type=jnp...  17.3 us
    dot_general x4, matrix products, row_step(): jnp.einsum('ihc,hjc->hij', grads, val_heads, preferred_element_type=jnp.f...  15.1 us
  transfers between devices with their start and end apart: 3, of which 3 were waited for; matrix products, arithmetic and copies ran while one was open for 4% of the time, Pallas kernels for 0%

profile of v1, /device:TPU:2, one launch (start us, length us, event | category | flops | bytes accessed | tf_op | source)
XLA Modules:
  0.0 696.9 jit_solution(11496993914123666168)
XLA Ops:
  7.9 102.3 %reduce-scatter.3.cloned.1.call-done = f32[1,1,32,2048]{3,2,1,0:T(8,128)} async-done(((f32[1,8,32,2048]{3,2,1,0:T(8,128)}), f32[1,1,32,2048]{3,2,1,0:T(8,128)}) %reduce-scatter.3.cloned.1.call-update) | async-done | bytes 262160 | tf_op jit(solution)/shard_map/reduce_scatter | solution.py:18
  112.2 6.1 stack.5
  118.3 5.2 all-to-all-start
  129.1 3.9 copy.29
  133.0 3.9 copy.32
  137.0 261.6 %all-to-all-done = bf16[32,3,32,2048]{3,2,1,0:T(8,128)(2,1)} async-done(((bf16[32,3,32,2048]{3,2,1,0:T(8,128)(2,1)}), bf16[32,3,32,2048]{3,2,1,0:T(8,128)(2,1)}, u32[]{:S(2)}, u32[]{:S(2)}) %all-to-all-start) | async-done | bytes 12582944 | tf_op jit(solution)/shard_map/all_to_all | solution.py:12
  398.6 6.2 copy.27
  404.8 6.5 copy.43
  411.3 4.1 broadcast_in_dim.30
  415.4 106.5 %while.15 = (s32[]{:T(128)}, f32[16,512,128]{2,1,0:T(8,128)}, f32[16,512,128]{2,1,0:T(8,128)}, f32[1024,16,128]{2,0,1:T(8,128)}, s32[4]{0:T(128)S(1)}, /*index=5...) while((s32[]{:T(128)}, f32[16,512,128]{2,1,0:T(8,128)}, ...), condition=%wide.region_3.4_spmd.clone, body=%wide.region_1.3_spmd.clone.sunk | while | flops 2712276992 | bytes 86482224 | solution.py:77
  426.2 5.0 select_add_fusion.5
  434.9 4.3 fusion.42
  450.0 6.6 select_add_fusion.5
  456.6 5.8 select_add_fusion.4
  462.5 4.3 fusion.42
  477.6 6.6 select_add_fusion.5
  484.2 5.8 select_add_fusion.4
  490.0 4.4 fusion.42
  505.3 6.6 select_add_fusion.5
  511.9 5.8 select_add_fusion.4
  517.7 4.2 fusion.42
  521.9 7.8 %copy_bitcast_fusion.7 = f32[1024,2048]{1,0:T(8,128)} fusion(f32[1024,16,128]{2,0,1:T(8,128)} %get-tuple-element.64), kind=kLoop, calls=%fused_computation.35 | loop fusion | flops 2097152 | bytes 16777216 | tf_op jit(solution)/shard_map/mul | solution.py:84
  529.8 5.9 fusion.19
  544.6 143.8 %reduce-scatter.5.cloned.1.call-done = f32[32,2048]{1,0:T(8,128)} async-done(((f32[1024,2048]{1,0:T(8,128)}), f32[32,2048]{1,0:T(8,128)}) %reduce-scatter.5.cloned.1.call-update) | async-done | bytes 262160 | tf_op jit(solution)/shard_map/reduce_scatter | solution.py:83
  (68 shorter events, 63.2 us)
Async XLA Ops:
  7.2 129.8 %copy-start = (s32[1,8]{1,0:T(1,128)S(1)}, s32[1,8]{1,0:T(1,128)}, u32[]{:S(2)}) copy-start(s32[1,8]{1,0:T(1,128)} %param.14) | copy-start | bytes 100
  7.2 103.0 %reduce-scatter.3.cloned.1.call-start = ((), (), s32[]{:S(2)}) async-start(), calls=%async_computation.3 | async-start | bytes 2359296 | tf_op jit(solution)/shard_map/reduce_scatter | solution.py:18
  118.3 5.3 copy-start.2
  118.3 280.4 %all-to-all-start = ((bf16[32,3,32,2048]{3,2,1,0:T(8,128)(2,1)}), bf16[32,3,32,2048]{3,2,1,0:T(8,128)(2,1)}, u32[]{:S(2)}, u32[]{:S(2)}) async-start(bf16[32,3,32,2048]{3,2,1,0:T(8,128)(2,1)} %stack.5), calls=%async_computation.1 | async-start | bytes 25165824 | tf_op jit(solution)/shard_map/all_to_all | solution.py:12
  123.5 564.9 %reduce-scatter.5.cloned.1.call-start = ((), (), s32[]{:S(2)}) async-start(), calls=%async_computation.4 | async-start | bytes 8650752 | tf_op jit(solution)/shard_map/reduce_scatter | solution.py:83
  420.8 1.6 copy-start.3
  444.6 1.6 copy-start.3
  472.2 1.6 copy-start.3
  499.9 1.6 copy-start.3
  539.3 150.7 %copy-start.1 = (s32[1,8]{1,0:T(1,128)S(1)}, s32[1,8]{1,0:T(1,128)}, u32[]{:S(2)}) copy-start(s32[1,8]{1,0:T(1,128)} %param.14) | copy-start | bytes 100
Sparse Core Ops, SparseCore 0:
  12.1 98.0 reduce-scatter.2
  529.9 158.4 reduce-scatter.4
